TPU v7x, 32 devices: a whole 2x2x4 slice. The times are simulated.
32 devices in a mesh: gx: 8 (over z, x), gy: 4 (over y, core).
Axes of the slice: x: 2, y: 2, z: 4, core: 2. Of those that a mesh axis runs over, the one named last changes fastest.
Arguments:
- velocity: float32 [3, 64, 256, 128], P(None, 'gx', 'gy'), may hold values from -2 to 3, as said below
- counts: int32 [8, 4, 9], P('gx', 'gy'), may hold values from 1 to 1024, as said below
- src_cell: int32 [8, 4, 9, 1024], P('gx', 'gy'), may hold values from 0 to 65535
- weights: float32 [8, 4, 9, 1024], P('gx', 'gy'), may hold values from 0.05 to 0.35
- dst_cell: int32 [8, 4, 9, 1024], P('gx', 'gy'), may hold values from 0 to 65535
- blade_tile: int32 [20, 192], replicated, may hold values from 0 to 31, as said below
- blade_cell: int32 [20, 192], replicated, may hold values from 0 to 65535
- blade_coef: float32 [20, 192], replicated, may hold values from 0.5 to 2
Outputs:
- updated: float32 [3, 64, 256, 128], P(None, 'gx', 'gy')
- forcing: float32 [3, 64, 256, 128], P(None, 'gx', 'gy')
Inputs may be any that keep to these rules, and one draw needn't show every extreme that they name: The velocity components, streamwise with a mean near 1. `counts`: some list is full, with 1024 used slots. `blade_tile`: turbines stand near one spanwise row of tiles; a turbine's points lie in at most three tiles.
All inputs are finite; a program needn't handle non-finite values.
Results may differ from a plain program's by a relative error of at most 0.00002.
Values sent between devices are 32-bit elements; how exact they have to be, the bound alone decides.
No kernel may reach another device: no remote copies, remote signals or barrier semaphores. Data moves between devices by JAX's collectives and lax.ppermute only.
A program may use at most 256 MiB of HBM per device.

v0:
```python
import jax
import jax.numpy as jnp
from jax import lax
from jax.sharding import PartitionSpec as P


def padded_2(cells, sides, width):
    for axis, dim in sides:
        count = lax.axis_size(axis)
        head = lax.slice_in_dim(cells, 0, width, axis=dim)
        tail = lax.slice_in_dim(cells, cells.shape[dim] - width, cells.shape[dim], axis=dim)
        cells = jnp.concatenate(
            [
                lax.ppermute(tail, axis, [(i, (i + 1) % count) for i in range(count)]),
                cells,
                lax.ppermute(head, axis, [((i + 1) % count, i) for i in range(count)]),
            ],
            axis=dim,
        )
    return cells


def body(velocity, counts, src_cell, weights, dst_cell, blade_tile, blade_cell, blade_coef):
    components = velocity.shape[0]
    cells_x = velocity.shape[1]
    cells_y = velocity.shape[2]
    levels = velocity.shape[3]
    total_cells = cells_x * cells_y * levels
    flat_vel = velocity.reshape(components, total_cells)
    count_y = lax.axis_size("gy")
    index_x = lax.axis_index("gx")
    index_y = lax.axis_index("gy")
    my_tile = index_x * count_y + index_y
    sampled = jnp.take(flat_vel, blade_cell, axis=1)
    owned = (blade_tile == my_tile)[None]
    sampled = jnp.where(owned, sampled, jnp.zeros_like(sampled))
    points = blade_cell.shape[1]
    points_x = lax.psum(sampled[0], ("gx", "gy"))
    rotor_mean = jnp.sum(points_x, axis=1) / points
    forces = -blade_coef[None] * rotor_mean[None, :, None] * sampled
    forcing = (
        jnp.zeros((components, total_cells), jnp.float32)
        .at[:, blade_cell.reshape(-1)]
        .add(forces.reshape(components, -1))
    )
    capacity = src_cell.shape[-1]
    active = lax.broadcasted_iota(jnp.int32, (9, capacity), 1) < counts[0, 0][:, None]
    masked_w = jnp.where(active, weights[0, 0], jnp.zeros_like(weights[0, 0]))
    picked = jnp.take(flat_vel, src_cell[0, 0].reshape(-1), axis=1).reshape(components, 9, capacity)
    blocks = jnp.concatenate([picked * masked_w[None], masked_w[None]], axis=0)
    grid_blocks = blocks.reshape(4, 3, 3, capacity)
    bordered = padded_2(grid_blocks, (("gx", 1), ("gy", 2)), 1)
    arrived = bordered[:, ::-2, ::-2].reshape(4, 9, capacity)
    targets = dst_cell[0, 0].reshape(-1)
    totals = jnp.zeros((4, total_cells), jnp.float32).at[:, targets].add(arrived.reshape(4, -1))
    corrected = (1.0 - totals[3]) * flat_vel - totals[:3]
    field_now = corrected.reshape(components, cells_x, cells_y, levels)
    padded = padded_2(field_now, (("gx", 1), ("gy", 2)), 1)
    padded = jnp.pad(padded, ((0, 0), (0, 0), (0, 0), (1, 1)))
    center = padded[:, 1:-1, 1:-1, 1:-1]
    east_side = padded[:, 2:, 1:-1, 1:-1]
    west_side = padded[:, :-2, 1:-1, 1:-1]
    north_side = padded[:, 1:-1, 2:, 1:-1]
    south_side = padded[:, 1:-1, :-2, 1:-1]
    upper_side = padded[:, 1:-1, 1:-1, 2:]
    lower_side = padded[:, 1:-1, 1:-1, :-2]
    laplace = (
        east_side + west_side + north_side + south_side + upper_side + lower_side - 6.0 * center
    )
    advection = (
        center[0:1] * (east_side - west_side) * 0.5
        + center[1:2] * (north_side - south_side) * 0.5
        + center[2:3] * (upper_side - lower_side) * 0.5
    )
    forcing_field = forcing.reshape(components, cells_x, cells_y, levels)
    updated = center + 0.2 * (0.15 * laplace - advection + forcing_field)
    return (updated, forcing_field)


def solution(mesh):
    placed = (
        P(None, "gx", "gy", None),
        P("gx", "gy", None),
        P("gx", "gy", None, None),
        P("gx", "gy", None, None),
        P("gx", "gy", None, None),
        P(),
        P(),
        P(),
    )
    return jax.shard_map(
        body,
        mesh=mesh,
        in_specs=placed,
        out_specs=(P(None, "gx", "gy", None), P(None, "gx", "gy", None)),
        check_vma=False,
    )
```

profile of v0, /device:TPU:1, one launch (start us, length us, event | category | flops | bytes accessed | tf_op | source)
XLA Modules:
  0.0 389.9 jit_solution(10842976870287354699)
XLA Ops:
  0.6 17.6 %copy.47 = f32[3,8,64,128]{0,3,2,1:T(8,128)} copy(f32[3,8,64,128]{3,2,1,0:T(8,128)} %param.8) | data formatting | bytes 1572864 | tf_op args[0]
  18.3 41.5 %gather_fusion = f32[9216,3]{1,0:T(8,128)} fusion(f32[3,65536]{0,1:T(8,128)} %bitcast.38, s32[9216]{0:T(1024)S(1)} %broadcast_clamp_fusion), kind=kCustom, calls=%fused_computation | custom fusion | bytes 258048 | tf_op jit(solution)/shard_map/jit(_take)/gather | solution.py:49
  59.8 3.1 copy.48
  63.5 0.7 reduce.15
  64.7 2.1 collective-permute-start
  66.8 3.1 collective-permute-start.1
  70.1 16.8 %gather_fusion.1 = f32[3840,3]{1,0:T(8,128)S(1)} fusion(f32[3,65536]{0,1:T(8,128)} %bitcast.39, s32[4096]{0:T(1024)S(1)} %pad_clamp_fusion), kind=kCustom, calls=%fused_computation.1 | custom fusion | bytes 107520 | tf_op jit(solution)/shard_map/jit(_take)/gather | solution.py:34
  86.9 0.9 copy.56
  87.8 37.7 %psum.7 = f32[20,192]{1,0:T(8,128)S(1)} all-reduce(f32[20,192]{1,0:T(8,128)S(1)} %fusion.17), channel_id=1, replica_groups=mesh['gx'=8,'gy'=4] {'gx','gy'}, use_global_device_ids=true, to_apply=%region_1.2 | all-reduce | flops 3840 | bytes 30720 | tf_op jit(solution)/shard_map/psum | solution.py:38
  125.8 3.4 collective-permute-start.2
  129.6 1.8 collective-permute-done.2
  131.4 1.6 collective-permute-done.3
  133.2 3.0 copy.49
  136.2 62.9 %scatter_custom_fusion = f32[4,65536]{0,1:T(8,128)} fusion(s32[9216]{0:T(1024)S(1)} %bitcast.52, f32[9216,4]{1,0:T(8,128)} %copy.49, f32[]{:T(128)} %constant.18.clone.1), kind=kCustom, calls=%fused_computation.12 | custom fusion | flops 36864 | bytes 1049088 | tf_op jit(solution)/shard_map/scatter-add | solution.py:55
  199.1 20.3 %fusion = f32[65536]{0:T(1024)S(1)} fusion(f32[4,65536]{0,1:T(8,128)} %scatter_custom_fusion), kind=kLoop, calls=%fused_computation.9 | loop fusion | flops 65536 | bytes 524288 | tf_op jit(solution)/shard_map/sub | solution.py:56
  219.4 34.2 %slice_subtract_fusion = f32[3,65536]{0,1:T(8,128)} fusion(f32[4,65536]{0,1:T(8,128)} %scatter_custom_fusion, f32[65536]{0:T(1024)S(1)} %fusion, f32[3,8,64,128]{0,3,2,1:T(8,128)} %copy.47), kind=kLoop, calls=%fused_computation.7 | loop fusion | flops 393216 | bytes 2621440 | tf_op jit(solution)/shard_map/sub | solution.py:56
  253.6 19.5 %copy.59 = f32[3,8,64,128]{3,2,1,0:T(8,128)S(1)} copy(f32[3,8,64,128]{0,3,2,1:T(8,128)} %bitcast.37) | data formatting | bytes 1572864 | tf_op jit(solution)/shard_map/reshape | solution.py:57
  273.1 2.8 collective-permute-start.4
  276.0 37.5 %scatter_custom_fusion.1 = f32[3,65536]{0,1:T(8,128)} fusion(s32[3840]{0:T(1024)S(1)} %fusion.18, f32[]{:T(128)} %constant.18.clone.1, f32[3840,3]{1,0:T(8,128)S(1)} %gather_fusion.1, f32[]{:T(128)} %constant.22.clone.1, f32[3840]{0:T(1024)S(1)} %mul.117, pred[3840]{0:T(1024)(128)(4,1)S(1)} %broadcast_in_dim.77, pred[3840]{0:T(1024)(128)(4,1)S(1)} %broadcast_in_dim.75), kind=kCustom, calls=%fused_computation.10 | custom fusion | flops 46080 | bytes 2778624 | tf_op jit(solution)/shard_map/scatter-add | solution.py:44
  313.5 19.5 %copy.58 = f32[3,8,64,128]{3,2,1,0:T(8,128)S(1)} copy(f32[3,8,64,128]{0,3,2,1:T(8,128)} %bitcast.40) | data formatting | bytes 1572864 | tf_op jit(solution)/shard_map/reshape | solution.py:75
  333.1 1.7 collective-permute-start.7
  334.8 52.5 %slice_reduce_fusion.2 = (f32[65536]{0:T(1024)S(1)}, f32[65536]{0:T(1024)S(1)}, f32[65536]{0:T(1024)S(1)}) fusion(f32[3,65536]{0,1:T(8,128)} %slice_subtract_fusion), kind=kLoop, calls=%fused_computation.6 | loop fusion | bytes 1572864 | tf_op jit(solution)/shard_map/slice | solution.py:71
  387.3 0.8 select_maximum_fusion
  388.1 1.8 multiply_add_fusion
  (58 shorter events, 2.3 us)
Async XLA Ops:
  0.6 17.6 %copy-start.2 = (s32[1,1,9,1024]{3,1,2,0:T(1,128)S(1)}, s32[1,1,9,1024]{3,1,2,0:T(1,128)}, u32[]{:S(2)}) copy-start(s32[1,1,9,1024]{3,1,2,0:T(1,128)} %param.10) | copy-start | bytes 110596
  18.2 45.3 %copy-start.7 = (s32[1,1,9]{2,1,0:T(1,128)S(1)}, s32[1,1,9]{2,1,0:T(1,128)}, u32[]{:S(2)}) copy-start(s32[1,1,9]{2,1,0:T(1,128)} %param.9) | copy-start | bytes 112
  18.2 46.0 %copy-start.3 = (f32[1,1,9,1024]{3,1,2,0:T(1,128)S(1)}, f32[1,1,9,1024]{3,1,2,0:T(1,128)}, u32[]{:S(2)}) copy-start(f32[1,1,9,1024]{3,1,2,0:T(1,128)} %param.11) | copy-start | bytes 110596
  18.2 51.7 %copy-start.4 = (s32[1,1,9,1024]{3,1,2,0:T(1,128)S(1)}, s32[1,1,9,1024]{3,1,2,0:T(1,128)}, u32[]{:S(2)}) copy-start(s32[1,1,9,1024]{3,1,2,0:T(1,128)} %param.12) | copy-start | bytes 110596
  18.2 51.8 %copy-start.1 = (s32[20,192]{1,0:T(8,128)S(1)}, s32[20,192]{1,0:T(8,128)}, u32[]{:S(2)}) copy-start(s32[20,192]{1,0:T(8,128)} %param.14) | copy-start | bytes 46084
  59.8 28.0 %copy-start.6 = (s32[20,192]{1,0:T(8,128)S(1)}, s32[20,192]{1,0:T(8,128)}, u32[]{:S(2)}) copy-start(s32[20,192]{1,0:T(8,128)} %param.13) | copy-start | bytes 46084
  59.8 69.4 %copy-start.5 = (f32[20,192]{1,0:T(8,128)S(1)}, f32[20,192]{1,0:T(8,128)}, u32[]{:S(2)}) copy-start(f32[20,192]{1,0:T(8,128)} %param.15) | copy-start | bytes 46084
  64.7 61.0 %collective-permute-start = (f32[4,1,3,1024]{3,0,2,1:T(4,128)S(1)}, f32[4,1,3,1024]{3,0,2,1:T(4,128)S(1)}, u32[]{:S(2)}, u32[]{:S(2)}) collective-permute-start(f32[4,1,3,1024]{3,0,2,1:T(4,128)S(1)} %get-tuple-element.19), channel_id=1, source_target_pairs={{0,4},{4,8},{8,12},{12,16},{16,20},{20,24},{24,28},{28,0},{1,5},{5... | collective-permute-start | bytes 147464 | tf_op jit(solution)/shard_map/ppermute | solution.py:14
  66.8 58.9 %collective-permute-start.1 = (f32[4,1,3,1024]{3,0,2,1:T(4,128)S(1)}, f32[4,1,3,1024]{3,0,2,1:T(4,128)S(1)}, u32[]{:S(2)}, u32[]{:S(2)}) collective-permute-start(f32[4,1,3,1024]{3,0,2,1:T(4,128)S(1)} %get-tuple-element.20), channel_id=1, source_target_pairs={{4,0},{8,4},{12,8},{16,12},{20,16},{24,20},{28,24},{0,28},{5,1},{9... | collective-permute-start | bytes 147464 | tf_op jit(solution)/shard_map/ppermute | solution.py:16
  125.8 5.6 %collective-permute-start.2 = (f32[4,5,1,1024]{3,0,2,1:T(4,128)S(1)}, f32[4,5,1,1024]{3,0,2,1:T(4,128)S(1)}, u32[]{:S(2)}, u32[]{:S(2)}) collective-permute-start(f32[4,5,1,1024]{3,0,2,1:T(4,128)S(1)} %get-tuple-element.17), channel_id=1, source_target_pairs={{0,1},{1,2},{2,3},{3,0},{4,5},{5,6},{6,7},{7,4},{8,9},{9,10},{10,1... | collective-permute-start | bytes 245768 | tf_op jit(solution)/shard_map/ppermute | solution.py:14
  129.2 3.9 collective-permute-start.3
  273.1 59.8 %collective-permute-start.4 = (f32[3,1,64,128]{3,2,1,0:T(8,128)S(1)}, f32[3,1,64,128]{3,2,1,0:T(8,128)S(1)}, u32[]{:S(2)}, u32[]{:S(2)}) collective-permute-start(f32[3,1,64,128]{3,2,1,0:T(8,128)S(1)} %get-tuple-element.16), channel_id=1, source_target_pairs={{4,0},{8,4},{12,8},{16,12},{20,16},{24,20},{28,24},{0,28},{5,1},{9... | collective-permute-start | bytes 294920 | tf_op jit(solution)/shard_map/ppermute | solution.py:16
  276.0 57.0 %collective-permute-start.5 = (f32[3,1,64,128]{3,2,1,0:T(8,128)S(1)}, f32[3,1,64,128]{3,2,1,0:T(8,128)S(1)}, u32[]{:S(2)}, u32[]{:S(2)}) collective-permute-start(f32[3,1,64,128]{3,2,1,0:T(8,128)S(1)} %get-tuple-element.15), channel_id=1, source_target_pairs={{0,4},{4,8},{8,12},{12,16},{16,20},{20,24},{24,28},{28,0},{1,5},{5... | collective-permute-start | bytes 294920 | tf_op jit(solution)/shard_map/ppermute | solution.py:14
  333.0 55.2 %copy-start = (f32[3,8,64,128]{3,2,1,0:T(8,128)}, f32[3,8,64,128]{3,2,1,0:T(8,128)S(1)}, u32[]{:S(2)}) copy-start(f32[3,8,64,128]{3,2,1,0:T(8,128)S(1)} %copy.58) | copy-start | bytes 2359300
  333.0 54.3 %collective-permute-start.6 = (f32[3,10,1,128]{3,2,1,0:T(1,128)S(1)}, f32[3,10,1,128]{3,2,1,0:T(1,128)S(1)}, u32[]{:S(2)}, u32[]{:S(2)}) collective-permute-start(f32[3,10,1,128]{3,2,1,0:T(1,128)S(1)} %get-tuple-element.14), channel_id=1, source_target_pairs={{1,0},{2,1},{3,2},{0,3},{5,4},{6,5},{7,6},{4,7},{9,8},{10,9},{11,1... | collective-permute-start | bytes 46088 | tf_op jit(solution)/shard_map/ppermute | solution.py:16
  333.1 54.2 %collective-permute-start.7 = (f32[3,10,1,128]{3,2,1,0:T(1,128)S(1)}, f32[3,10,1,128]{3,2,1,0:T(1,128)S(1)}, u32[]{:S(2)}, u32[]{:S(2)}) collective-permute-start(f32[3,10,1,128]{3,2,1,0:T(1,128)S(1)} %get-tuple-element.13), channel_id=1, source_target_pairs={{0,1},{1,2},{2,3},{3,0},{4,5},{5,6},{6,7},{7,4},{8,9},{9,10},{10,1... | collective-permute-start | bytes 46088 | tf_op jit(solution)/shard_map/ppermute | solution.py:14
where the time goes:
time: 391 us; the launch traced here: 390 us
  local copies, waits for them, and re-layouts  175 us (45%)
  other arithmetic  159 us (41%)
  blocking collectives  37.7 us (10%)
  starting transfers between devices  13.2 us (3%)
    scatter-add x1, other arithmetic, body(): jnp.zeros((4, total_cells), jnp.float32).at[:, targets]  62.9 us
    sub x2, other arithmetic, body(): corrected = (1.0 - totals[3]) * flat_vel - totals[:3]  54.5 us
    slice x1, local copies, waits for them, and re-layouts, body(): center[0:1] * (east_side - west_side) * 0.5  52.5 us
    gather x2, local copies, waits for them, and re-layouts, body(): jnp.take(flat_vel, src_cell[0, 0].reshape(-1), axis=1)  44.6 us
    psum x1, blocking collectives, body(): points_x = lax.psum(sampled[0], ('gx', 'gy'))  37.7 us
    scatter-add x1, other arithmetic, body(): forcing = jnp.zeros((components, total_cells), jnp.float32).at[:, blade_c...  37.5 us
    reshape x1, local copies, waits for them, and re-layouts, body(): field_now = corrected.reshape(components, cells_x, cells_y, levels)  19.5 us
    reshape x1, local copies, waits for them, and re-layouts, body(): forcing_field = forcing.reshape(components, cells_x, cells_y, levels)  19.5 us
  transfers between devices with their start and end apart: 8, of which 2 were waited for; matrix products, arithmetic and copies ran while one was open for 33% of the time, Pallas kernels for 0%

commit v1 on v0

--- a/solution.py
+++ b/solution.py
@@ -35,7 +35,7 @@
     owned = (blade_tile == my_tile)[None]
     sampled = jnp.where(owned, sampled, jnp.zeros_like(sampled))
     points = blade_cell.shape[1]
-    points_x = lax.psum(sampled[0], ("gx", "gy"))
+    points_x = jnp.sum(lax.all_gather(sampled[0], ("gx", "gy")), axis=0)
     rotor_mean = jnp.sum(points_x, axis=1) / points
     forces = -blade_coef[None] * rotor_mean[None, :, None] * sampled
     forcing = (

time: 391 us -> 391 us (level)
  blocking collectives: 37.7 us -> 42.1 us
  starting transfers between devices: 13.2 us -> 9.06 us
    all_gather x0 -> x1, blocking collectives: none -> 42.1 us  [body(): points_x = jnp.sum(lax.all_gather(sampled[0], ('gx', 'gy')), axis=0)]
    psum x1 -> x0, blocking collectives: 37.7 us -> none  [body(): points_x = lax.psum(sampled[0], ('gx', 'gy'))]
where the time goes in v1:
time: 391 us; the launch traced here: 390 us
  local copies, waits for them, and re-layouts  175 us (45%)
  other arithmetic  159 us (41%)
  blocking collectives  42.1 us (11%)
  starting transfers between devices  9.06 us (2%)
    scatter-add x1, other arithmetic, body(): jnp.zeros((4, total_cells), jnp.float32).at[:, targets]  62.9 us
    sub x2, other arithmetic, body(): corrected = (1.0 - totals[3]) * flat_vel - totals[:3]  54.5 us
    slice x1, local copies, waits for them, and re-layouts, body(): center[0:1] * (east_side - west_side) * 0.5  52.5 us
    gather x2, local copies, waits for them, and re-layouts, body(): jnp.take(flat_vel, src_cell[0, 0].reshape(-1), axis=1)  44.6 us
    all_gather x1, blocking collectives, body(): points_x = jnp.sum(lax.all_gather(sampled[0], ('gx', 'gy')), axis=0)  42.1 us
    scatter-add x1, other arithmetic, body(): forcing = jnp.zeros((components, total_cells), jnp.float32).at[:, blade_c...  37.5 us
    reshape x1, local copies, waits for them, and re-layouts, body(): field_now = corrected.reshape(components, cells_x, cells_y, levels)  19.5 us
    reshape x1, local copies, waits for them, and re-layouts, body(): forcing_field = forcing.reshape(components, cells_x, cells_y, levels)  19.5 us
  transfers between devices with their start and end apart: 8, of which 2 were waited for; matrix products, arithmetic and copies ran while one was open for 33% of the time, Pallas kernels for 0%

profile of v1, /device:TPU:1, one launch (start us, length us, event | category | flops | bytes accessed | tf_op | source)
XLA Modules:
  0.0 390.1 jit_solution(1563077099298250468)
XLA Ops:
  0.6 17.6 %copy.45 = f32[3,8,64,128]{0,3,2,1:T(8,128)} copy(f32[3,8,64,128]{3,2,1,0:T(8,128)} %param.8) | data formatting | bytes 1572864 | tf_op args[0]
  18.3 41.5 %gather_fusion = f32[9216,3]{1,0:T(8,128)} fusion(f32[3,65536]{0,1:T(8,128)} %bitcast.36, s32[9216]{0:T(1024)S(1)} %broadcast_clamp_fusion), kind=kCustom, calls=%fused_computation | custom fusion | bytes 258048 | tf_op jit(solution)/shard_map/jit(_take)/gather | solution.py:49
  59.8 3.1 copy.46
  63.5 0.7 reduce.16
  64.7 2.1 collective-permute-start
  66.8 3.1 collective-permute-start.1
  70.1 16.8 %gather_fusion.1 = f32[3840,3]{1,0:T(8,128)S(1)} fusion(f32[3,65536]{0,1:T(8,128)} %bitcast.37, s32[4096]{0:T(1024)S(1)} %pad_clamp_fusion), kind=kCustom, calls=%fused_computation.1 | custom fusion | bytes 107520 | tf_op jit(solution)/shard_map/jit(_take)/gather | solution.py:34
  86.9 0.9 copy.54
  87.8 42.1 %all_gather.3 = f32[32,20,192]{2,1,0:T(8,128)S(1)} all-gather(f32[1,20,192]{2,1,0:T(8,128)S(1)} %fusion.16), channel_id=1, replica_groups=mesh['gx'=8,'gy'=4] {'gx','gy'}, dimensions={0}, use_global_device_ids=true | all-gather | bytes 506880 | tf_op jit(solution)/shard_map/all_gather | solution.py:38
  131.3 0.6 collective-permute-done.2
  131.8 2.7 collective-permute-done.3
  134.7 3.0 copy.47
  137.7 62.9 %scatter_custom_fusion = f32[4,65536]{0,1:T(8,128)} fusion(s32[9216]{0:T(1024)S(1)} %bitcast.50, f32[9216,4]{1,0:T(8,128)} %copy.47, f32[]{:T(128)} %constant.18.clone.1), kind=kCustom, calls=%fused_computation.12 | custom fusion | flops 36864 | bytes 1049088 | tf_op jit(solution)/shard_map/scatter-add | solution.py:55
  200.6 20.3 %fusion = f32[65536]{0:T(1024)S(1)} fusion(f32[4,65536]{0,1:T(8,128)} %scatter_custom_fusion), kind=kLoop, calls=%fused_computation.9 | loop fusion | flops 65536 | bytes 524288 | tf_op jit(solution)/shard_map/sub | solution.py:56
  220.9 34.2 %slice_subtract_fusion = f32[3,65536]{0,1:T(8,128)} fusion(f32[4,65536]{0,1:T(8,128)} %scatter_custom_fusion, f32[65536]{0:T(1024)S(1)} %fusion, f32[3,8,64,128]{0,3,2,1:T(8,128)} %copy.45), kind=kLoop, calls=%fused_computation.7 | loop fusion | flops 393216 | bytes 2621440 | tf_op jit(solution)/shard_map/sub | solution.py:56
  255.1 19.5 %copy.57 = f32[3,8,64,128]{3,2,1,0:T(8,128)S(1)} copy(f32[3,8,64,128]{0,3,2,1:T(8,128)} %bitcast.35) | data formatting | bytes 1572864 | tf_op jit(solution)/shard_map/reshape | solution.py:57
  274.7 1.5 collective-permute-start.5
  276.2 37.5 %scatter_custom_fusion.1 = f32[3,65536]{0,1:T(8,128)} fusion(s32[3840]{0:T(1024)S(1)} %fusion.17, f32[]{:T(128)} %constant.18.clone.1, f32[3840,3]{1,0:T(8,128)S(1)} %gather_fusion.1, f32[]{:T(128)} %constant.22.clone.1, f32[3840]{0:T(1024)S(1)} %mul.117, pred[3840]{0:T(1024)(128)(4,1)S(1)} %broadcast_in_dim.77, pred[3840]{0:T(1024)(128)(4,1)S(1)} %broadcast_in_dim.75), kind=kCustom, calls=%fused_computation.10 | custom fusion | flops 46080 | bytes 2778624 | tf_op jit(solution)/shard_map/scatter-add | solution.py:44
  313.7 19.5 %copy.56 = f32[3,8,64,128]{3,2,1,0:T(8,128)S(1)} copy(f32[3,8,64,128]{0,3,2,1:T(8,128)} %bitcast.38) | data formatting | bytes 1572864 | tf_op jit(solution)/shard_map/reshape | solution.py:75
  333.2 0.8 collective-permute-start.6
  334.0 1.0 collective-permute-start.7
  335.0 52.5 %slice_reduce_fusion.2 = (f32[65536]{0:T(1024)S(1)}, f32[65536]{0:T(1024)S(1)}, f32[65536]{0:T(1024)S(1)}) fusion(f32[3,65536]{0,1:T(8,128)} %slice_subtract_fusion), kind=kLoop, calls=%fused_computation.6 | loop fusion | bytes 1572864 | tf_op jit(solution)/shard_map/slice | solution.py:71
  387.5 0.8 select_maximum_fusion
  388.3 1.8 multiply_add_fusion
  (58 shorter events, 2.9 us)
Async XLA Ops:
  0.6 17.6 %copy-start.2 = (s32[1,1,9,1024]{3,1,2,0:T(1,128)S(1)}, s32[1,1,9,1024]{3,1,2,0:T(1,128)}, u32[]{:S(2)}) copy-start(s32[1,1,9,1024]{3,1,2,0:T(1,128)} %param.10) | copy-start | bytes 110596
  18.2 45.3 %copy-start.7 = (s32[1,1,9]{2,1,0:T(1,128)S(1)}, s32[1,1,9]{2,1,0:T(1,128)}, u32[]{:S(2)}) copy-start(s32[1,1,9]{2,1,0:T(1,128)} %param.9) | copy-start | bytes 112
  18.2 46.0 %copy-start.3 = (f32[1,1,9,1024]{3,1,2,0:T(1,128)S(1)}, f32[1,1,9,1024]{3,1,2,0:T(1,128)}, u32[]{:S(2)}) copy-start(f32[1,1,9,1024]{3,1,2,0:T(1,128)} %param.11) | copy-start | bytes 110596
  18.2 51.7 %copy-start.4 = (s32[1,1,9,1024]{3,1,2,0:T(1,128)S(1)}, s32[1,1,9,1024]{3,1,2,0:T(1,128)}, u32[]{:S(2)}) copy-start(s32[1,1,9,1024]{3,1,2,0:T(1,128)} %param.12) | copy-start | bytes 110596
  18.2 51.8 %copy-start.1 = (s32[20,192]{1,0:T(8,128)S(1)}, s32[20,192]{1,0:T(8,128)}, u32[]{:S(2)}) copy-start(s32[20,192]{1,0:T(8,128)} %param.14) | copy-start | bytes 46084
  59.8 28.0 %copy-start.6 = (s32[20,192]{1,0:T(8,128)S(1)}, s32[20,192]{1,0:T(8,128)}, u32[]{:S(2)}) copy-start(s32[20,192]{1,0:T(8,128)} %param.13) | copy-start | bytes 46084
  59.8 71.0 %copy-start.5 = (f32[20,192]{1,0:T(8,128)S(1)}, f32[20,192]{1,0:T(8,128)}, u32[]{:S(2)}) copy-start(f32[20,192]{1,0:T(8,128)} %param.15) | copy-start | bytes 46084
  64.7 65.4 %collective-permute-start = (f32[4,1,3,1024]{3,0,2,1:T(4,128)S(1)}, f32[4,1,3,1024]{3,0,2,1:T(4,128)S(1)}, u32[]{:S(2)}, u32[]{:S(2)}) collective-permute-start(f32[4,1,3,1024]{3,0,2,1:T(4,128)S(1)} %get-tuple-element.19), channel_id=1, source_target_pairs={{0,4},{4,8},{8,12},{12,16},{16,20},{20,24},{24,28},{28,0},{1,5},{5... | collective-permute-start | bytes 147464 | tf_op jit(solution)/shard_map/ppermute | solution.py:14
  66.8 63.4 %collective-permute-start.1 = (f32[4,1,3,1024]{3,0,2,1:T(4,128)S(1)}, f32[4,1,3,1024]{3,0,2,1:T(4,128)S(1)}, u32[]{:S(2)}, u32[]{:S(2)}) collective-permute-start(f32[4,1,3,1024]{3,0,2,1:T(4,128)S(1)} %get-tuple-element.20), channel_id=1, source_target_pairs={{4,0},{8,4},{12,8},{16,12},{20,16},{24,20},{28,24},{0,28},{5,1},{9... | collective-permute-start | bytes 147464 | tf_op jit(solution)/shard_map/ppermute | solution.py:16
  130.3 1.5 collective-permute-start.2
  130.3 4.2 %collective-permute-start.3 = (f32[4,5,1,1024]{3,0,2,1:T(4,128)S(1)}, f32[4,5,1,1024]{3,0,2,1:T(4,128)S(1)}, u32[]{:S(2)}, u32[]{:S(2)}) collective-permute-start(f32[4,5,1,1024]{3,0,2,1:T(4,128)S(1)} %get-tuple-element.18), channel_id=1, source_target_pairs={{1,0},{2,1},{3,2},{0,3},{5,4},{6,5},{7,6},{4,7},{9,8},{10,9},{11,1... | collective-permute-start | bytes 245768 | tf_op jit(solution)/shard_map/ppermute | solution.py:16
  274.6 58.5 %collective-permute-start.4 = (f32[3,1,64,128]{3,2,1,0:T(8,128)S(1)}, f32[3,1,64,128]{3,2,1,0:T(8,128)S(1)}, u32[]{:S(2)}, u32[]{:S(2)}) collective-permute-start(f32[3,1,64,128]{3,2,1,0:T(8,128)S(1)} %get-tuple-element.16), channel_id=1, source_target_pairs={{4,0},{8,4},{12,8},{16,12},{20,16},{24,20},{28,24},{0,28},{5,1},{9... | collective-permute-start | bytes 294920 | tf_op jit(solution)/shard_map/ppermute | solution.py:16
  274.7 58.5 %collective-permute-start.5 = (f32[3,1,64,128]{3,2,1,0:T(8,128)S(1)}, f32[3,1,64,128]{3,2,1,0:T(8,128)S(1)}, u32[]{:S(2)}, u32[]{:S(2)}) collective-permute-start(f32[3,1,64,128]{3,2,1,0:T(8,128)S(1)} %get-tuple-element.15), channel_id=1, source_target_pairs={{0,4},{4,8},{8,12},{12,16},{16,20},{20,24},{24,28},{28,0},{1,5},{5... | collective-permute-start | bytes 294920 | tf_op jit(solution)/shard_map/ppermute | solution.py:14
  333.1 55.2 %copy-start = (f32[3,8,64,128]{3,2,1,0:T(8,128)}, f32[3,8,64,128]{3,2,1,0:T(8,128)S(1)}, u32[]{:S(2)}) copy-start(f32[3,8,64,128]{3,2,1,0:T(8,128)S(1)} %copy.56) | copy-start | bytes 2359300
  333.2 54.3 %collective-permute-start.6 = (f32[3,10,1,128]{3,2,1,0:T(1,128)S(1)}, f32[3,10,1,128]{3,2,1,0:T(1,128)S(1)}, u32[]{:S(2)}, u32[]{:S(2)}) collective-permute-start(f32[3,10,1,128]{3,2,1,0:T(1,128)S(1)} %get-tuple-element.14), channel_id=1, source_target_pairs={{1,0},{2,1},{3,2},{0,3},{5,4},{6,5},{7,6},{4,7},{9,8},{10,9},{11,1... | collective-permute-start | bytes 46088 | tf_op jit(solution)/shard_map/ppermute | solution.py:16
  334.0 53.5 %collective-permute-start.7 = (f32[3,10,1,128]{3,2,1,0:T(1,128)S(1)}, f32[3,10,1,128]{3,2,1,0:T(1,128)S(1)}, u32[]{:S(2)}, u32[]{:S(2)}) collective-permute-start(f32[3,10,1,128]{3,2,1,0:T(1,128)S(1)} %get-tuple-element.13), channel_id=1, source_target_pairs={{0,1},{1,2},{2,3},{3,0},{4,5},{5,6},{6,7},{7,4},{8,9},{9,10},{10,1... | collective-permute-start | bytes 46088 | tf_op jit(solution)/shard_map/ppermute | solution.py:14
